TPU v7x, 32 devices: a whole 2x2x4 slice. The times are simulated.
32 devices in a mesh: ch: 4 (over z), ha: 2 (over x), dp: 4 (over y, core).
Axes of the slice: x: 2, y: 2, z: 4, core: 2. Of those that a mesh axis runs over, the one named last changes fastest.
Arguments:
- features: bfloat16 [384, 4, 4, 4, 128], P('ch', 'dp', None, 'ha'), may hold values from -26 to 26
- frame_count: int32 [4], P('dp'), may hold values from 1 to 4, as said below
- norm1_gain: float32 [384], P('ch'), may hold values from 0.5 to 2
- norm1_shift: float32 [384], P('ch'), may hold values from -3 to 3
- qkv_weight: bfloat16 [384, 1152], replicated, may hold values from -0.51031036 to 0.51031036
- qkv_bias: float32 [1152], replicated, may hold values from -3 to 3
- out_weight: bfloat16 [384, 384], replicated, may hold values from -0.3125 to 0.3125
- out_bias: float32 [384], replicated, may hold values from -3 to 3
- norm2_gain: float32 [384], P('ch'), may hold values from 0.5 to 2
- norm2_shift: float32 [384], P('ch'), may hold values from -3 to 3
- conv_weight: bfloat16 [3, 3, 3, 384, 384], P(None, None, None, 'ch'), may hold values from -0.0625 to 0.0625
- conv_bias: float32 [384], P('ch'), may hold values from -3 to 3
- cotangent: bfloat16 [384, 4, 4, 4, 128], P('ch', 'dp', None, 'ha'), may hold values from -0.0625 to 0.0625
Outputs:
- mixed: bfloat16 [384, 4, 4, 4, 128], P('ch', 'dp', None, 'ha')
- weight_grad: float32 [3, 3, 3, 384, 384], P(None, None, None, 'ch')
Inputs may be any that keep to these rules, and one draw needn't show every extreme that they name: `frame_count`: some clip has all 4 frames valid and some clip only one.
All inputs are finite; a program needn't handle non-finite values.
Results may differ from a plain program's by a relative error of at most 0.015.
Values may be sent and summed in bfloat16 or wider, within the bound.
A program may use at most 64 MiB of HBM per device.

v0:
```python
import jax
import jax.numpy as jnp
from jax import lax
from jax.sharding import PartitionSpec as P

GROUPS = 32
EPS = 1e-06


def padded_2(x, sides, width):
    for axis, dim in sides:
        count, length = (lax.axis_size(axis), x.shape[dim])
        up = [(i, (i + 1) % count) for i in range(count - 1)]
        down = [(j, i) for i, j in up]
        last = lax.slice_in_dim(x, length - width, length, axis=dim)
        leading = lax.slice_in_dim(x, 0, width, axis=dim)
        before = lax.ppermute(last, axis, up)
        after = lax.ppermute(leading, axis, down)
        x = jnp.concatenate([before, x, after], axis=dim)
    return x


def frame_mask(frame_count, frames):
    position = lax.broadcasted_iota(jnp.int32, (frame_count.shape[0], frames), 1)
    return (position < frame_count[:, None]).astype(jnp.float32)


def moments(values, mask, groups):
    chans, clips, frames, rows, cols = values.shape
    data = values.astype(jnp.float32).reshape(groups, chans // groups, clips, frames, rows * cols)
    first = jnp.einsum("gkbfp,bf->gb", data, mask)
    second = jnp.einsum("gkbfp,bf->gb", data * data, mask)
    return (first, second)


def normalize(values, first, second, count, gain, shift, groups):
    chans, clips, frames, rows, cols = values.shape
    mean = first / count[None, :]
    var = second / count[None, :] - mean * mean
    scale = lax.rsqrt(var + EPS)
    data = values.astype(jnp.float32).reshape(groups, chans // groups, clips, frames, rows * cols)
    normed = (data - mean[:, None, :, None, None]) * scale[:, None, :, None, None]
    normed = normed.reshape(values.shape)
    return normed * gain[:, None, None, None, None] + shift[:, None, None, None, None]


def attend(carry, queries, keys, values, scale):
    top, total, acc = carry
    scores = jnp.einsum("itc,isc->its", queries, keys, preferred_element_type=jnp.float32) * scale
    new_top = jnp.max(scores, axis=2)
    factor = jnp.exp(top - new_top)
    weights = jnp.exp(scores - new_top[..., None])
    total = total * factor + jnp.sum(weights, axis=2)
    acc = acc * factor[..., None] + jnp.einsum(
        "its,isc->itc", weights.astype(jnp.bfloat16), values, preferred_element_type=jnp.float32
    )
    return (new_top, total, acc)


def tap_stack(padded, time_tap, frames, rows, cols):
    windows = []
    for row_tap in range(3):
        for col_tap in range(3):
            windows.append(
                padded[
                    :,
                    :,
                    time_tap : time_tap + frames,
                    row_tap : row_tap + rows,
                    col_tap : col_tap + cols,
                ]
            )
    return jnp.concatenate(windows, axis=0)


def body(
    features,
    frame_count,
    norm1_gain,
    norm1_shift,
    qkv_weight,
    qkv_bias,
    out_weight,
    out_bias,
    norm2_gain,
    norm2_shift,
    conv_weight,
    conv_bias,
    cotangent,
):
    chans, clips, frames, rows, cols = features.shape
    groups = GROUPS // lax.axis_size("ch")
    mask = frame_mask(frame_count, frames)
    count = frame_count.astype(jnp.float32) * (chans // groups * rows * lax.axis_size("ha") * cols)
    first, second = moments(features, mask, groups)
    first, second = lax.psum((first, second), "ha")
    normed = normalize(features, first, second, count, norm1_gain, norm1_shift, groups).astype(
        jnp.bfloat16
    )
    by_frame = lax.all_to_all(normed, "ch", split_axis=2, concat_axis=0, tiled=True)
    width = by_frame.shape[0]
    items = clips * by_frame.shape[2]
    tok_rows = rows * cols
    tokens = by_frame.reshape(width, items, tok_rows)
    queries = lax.dot_general(
        tokens, qkv_weight[:, :width], (((0,), (0,)), ((), ())), preferred_element_type=jnp.float32
    )
    queries = (queries + qkv_bias[:width]).astype(jnp.bfloat16)
    scale = width ** (-0.5)
    start_carry = (
        jnp.full((items, tok_rows), -jnp.inf, jnp.float32),
        jnp.zeros((items, tok_rows), jnp.float32),
        jnp.zeros((items, tok_rows, width), jnp.float32),
    )
    pairs = lax.dot_general(
        tokens, qkv_weight[:, width:], (((0,), (0,)), ((), ())), preferred_element_type=jnp.float32
    )
    pairs = (pairs + qkv_bias[width:]).astype(jnp.bfloat16)
    piece = lax.all_gather(pairs, "ha", axis=1, tiled=True)
    top, total, acc = attend(start_carry, queries, piece[..., :width], piece[..., width:], scale)
    attended = (acc / total[..., None]).astype(jnp.bfloat16)
    projected = lax.dot_general(
        out_weight, attended, (((0,), (2,)), ((), ())), preferred_element_type=jnp.float32
    )
    projected = (projected + out_bias[:, None, None]).astype(jnp.bfloat16).reshape(by_frame.shape)
    update = lax.all_to_all(projected, "ch", split_axis=0, concat_axis=2, tiled=True)
    hidden = (features.astype(jnp.float32) + update.astype(jnp.float32)).astype(jnp.bfloat16)
    first, second = moments(hidden, mask, groups)
    first, second = lax.psum((first, second), "ha")
    gated = jax.nn.silu(
        normalize(hidden, first, second, count, norm2_gain, norm2_shift, groups)
    ).astype(jnp.bfloat16)
    with_rows = padded_2(gated, (("ha", 3),), 1)
    padded = jnp.pad(with_rows, ((0, 0), (0, 0), (2, 0), (0, 0), (1, 1)))
    stacks = [tap_stack(padded, time_tap, frames, rows, cols) for time_tap in range(3)]
    amount = chans * lax.axis_size("ch")
    summed = jnp.zeros((amount, clips, frames, rows, cols), jnp.float32)
    for time_tap in range(3):
        part = conv_weight[time_tap].reshape(9 * chans, amount)
        summed = summed + lax.dot_general(
            part, stacks[time_tap], (((0,), (0,)), ((), ())), preferred_element_type=jnp.float32
        )
    conv_out = lax.psum_scatter(
        summed.astype(jnp.bfloat16), "ch", scatter_dimension=0, tiled=True
    ).astype(jnp.float32)
    mixed = mask[None, :, :, None, None] * (
        hidden.astype(jnp.float32) + conv_out + conv_bias[:, None, None, None, None]
    )
    mixed = mixed.astype(jnp.bfloat16)
    masked_cot = cotangent * mask.astype(jnp.bfloat16)[None, :, :, None, None]
    full_width = chans * lax.axis_size("ch")
    carry = jnp.zeros((3, 9 * chans, full_width), jnp.float32)
    piece = lax.all_gather(masked_cot, "ch", axis=0, tiled=True)
    start = jnp.int32(0)
    for time_tap in range(3):
        part = lax.dot_general(
            stacks[time_tap],
            piece,
            (((1, 2, 3, 4), (1, 2, 3, 4)), ((), ())),
            preferred_element_type=jnp.float32,
        )
        carry = lax.dynamic_update_slice(
            carry, part[None], (jnp.int32(time_tap), jnp.int32(0), start)
        )
    grad_table = carry
    grad_table = grad_table.reshape(3, 3, 3, chans, full_width)
    weight_grad = lax.psum(grad_table.astype(jnp.bfloat16), ("ha", "dp")).astype(jnp.float32)
    return (mixed, weight_grad)


def solution(mesh):
    placed = (
        P("ch", "dp", None, "ha", None),
        P("dp"),
        P("ch"),
        P("ch"),
        P(),
        P(),
        P(),
        P(),
        P("ch"),
        P("ch"),
        P(None, None, None, "ch", None),
        P("ch"),
        P("ch", "dp", None, "ha", None),
    )
    return jax.shard_map(
        body,
        mesh=mesh,
        in_specs=placed,
        out_specs=(P("ch", "dp", None, "ha", None), P(None, None, None, "ch", None)),
        check_vma=False,
    )
```

profile of v0, /device:TPU:0, one launch (start us, length us, event | category | flops | bytes accessed | tf_op | source)
XLA Modules:
  0.0 170.4 jit_solution(4983406673391585404)
XLA Ops:
  8.7 1.1 fusion.57
  10.4 5.9 %all-reduce.3 = (f32[8,1]{0,1:T(1,128)S(1)}, f32[8,1]{0,1:T(1,128)S(1)}) all-reduce(f32[8,1]{0,1:T(1,128)S(1)} %convolution_bitcast_fusion.3, f32[8,1]{0,1:T(1,128)S(1)} %convolution_bitcast_fusion.2), channel_id=1, replica_groups=mesh['ch'=4,'ha'=2,'dp'=4] {'ha'}, use_global_device_ids=true, to_apply=%region_2.0 | all-reduce | flops 16 | bytes 128 | tf_op jit(solution)/shard_map/psum | solution.py:96
  16.6 1.8 %fusion.78 = bf16[96,1,4,2,128]{4,0,3,1,2:T(8,128)(2,1)} fusion(f32[96]{0:T(128)} %param.16, f32[96]{0:T(128)} %param.15, f32[96]{0:T(128)S(1)} %mul.117, f32[96]{0:T(128)S(1)} %sub.66, bf16[96,1,4,2,128]{4,3,2,1,0:T(2,128)(2,1)} %param.13), kind=kLoop, calls=%fused_computation.84 | loop fusion | flops 589824 | bytes 394752 | tf_op jit(solution)/shard_map/convert_element_type | solution.py:97
  18.4 5.5 %all-to-all-start = ((bf16[96,1,4,2,128]{4,0,3,1,2:T(8,128)(2,1)}), bf16[96,1,4,2,128]{4,0,3,1,2:T(8,128)(2,1)S(1)}, u32[]{:S(2)}, u32[]{:S(2)}) async-start(bf16[96,1,4,2,128]{4,0,3,1,2:T(8,128)(2,1)} %fusion.78), calls=%async_computation | async-start | bytes 393216 | tf_op jit(solution)/shard_map/all_to_all | solution.py:100
  24.0 0.7 slice.120
  24.7 5.5 %all-to-all-done = bf16[96,1,4,2,128]{4,0,3,1,2:T(8,128)(2,1)S(1)} async-done(((bf16[96,1,4,2,128]{4,0,3,1,2:T(8,128)(2,1)}), bf16[96,1,4,2,128]{4,0,3,1,2:T(8,128)(2,1)S(1)}, u32[]{:S(2)}, u32[]{:S(2)}) %all-to-all-start) | async-done | bytes 196640 | tf_op jit(solution)/shard_map/all_to_all | solution.py:100
  30.4 1.5 fusion.37
  31.8 8.9 %all-gather = bf16[512,768]{1,0:T(8,128)(2,1)S(1)} all-gather(bf16[256,768]{1,0:T(8,128)(2,1)S(1)} %fusion.37), channel_id=2, replica_groups=mesh['ch'=4,'ha'=2,'dp'=4] {'ha'}, dimensions={0}, use_global_device_ids=true | all-gather | bytes 1179648 | tf_op jit(solution)/shard_map/all_gather | solution.py:119
  40.8 1.6 fusion.104
  42.7 0.6 fusion.46
  43.3 0.9 copy.33
  44.1 3.5 %all-to-all-start.1 = ((bf16[384,1,1,2,128]{4,3,2,1,0:T(2,128)(2,1)}), bf16[384,1,1,2,128]{4,3,2,1,0:T(2,128)(2,1)S(1)}, u32[]{:S(2)}, u32[]{:S(2)}) async-start(bf16[384,1,1,2,128]{4,3,2,1,0:T(2,128)(2,1)} %copy.33), calls=%async_computation.1 | async-start | bytes 393216 | tf_op jit(solution)/shard_map/all_to_all | solution.py:126
  47.8 6.1 %all-to-all-done.1 = bf16[384,1,1,2,128]{4,3,2,1,0:T(2,128)(2,1)S(1)} async-done(((bf16[384,1,1,2,128]{4,3,2,1,0:T(2,128)(2,1)}), bf16[384,1,1,2,128]{4,3,2,1,0:T(2,128)(2,1)S(1)}, u32[]{:S(2)}, u32[]{:S(2)}) %all-to-all-start.1) | async-done | bytes 196640 | tf_op jit(solution)/shard_map/all_to_all | solution.py:126
  54.8 17.3 %all_gather.7 = bf16[384,1,4,2,128]{4,0,3,2,1:T(8,128)(2,1)} all-gather(bf16[96,1,4,2,128]{4,0,3,2,1:T(8,128)(2,1)S(1)} %copy_multiply_fusion), channel_id=1, replica_groups=mesh['ch'=4,'ha'=2,'dp'=4] {'ch'}, dimensions={0}, use_global_device_ids=true | all-gather | bytes 983040 | tf_op jit(solution)/shard_map/all_gather | solution.py:153
  72.1 4.9 %all-reduce.2 = (f32[8,1]{0,1:T(1,128)S(1)}, f32[8,1]{0,1:T(1,128)S(1)}) all-reduce(f32[8,1]{0,1:T(1,128)S(1)} %convolution_bitcast_fusion.1, f32[8,1]{0,1:T(1,128)S(1)} %convolution_bitcast_fusion), channel_id=1, replica_groups=mesh['ch'=4,'ha'=2,'dp'=4] {'ha'}, use_global_device_ids=true, to_apply=%region_10.11 | all-reduce | flops 16 | bytes 128 | tf_op jit(solution)/shard_map/psum | solution.py:129
  77.7 3.4 %collective-permute-start = (bf16[96,1,4,1,128]{4,0,3,2,1:T(8,128)(2,1)S(1)}, bf16[96,1,4,1,128]{4,0,3,2,1:T(8,128)(2,1)S(1)}, u32[]{:S(2)}, u32[]{:S(2)}) collective-permute-start(bf16[96,1,4,1,128]{4,0,3,2,1:T(8,128)(2,1)S(1)} %get-tuple-element.47), channel_id=1, source_target_pairs={{0,4},{1,5},{2,6},{3,7},{8,12},{9,13},{10,14},{11,15},{16,20},{17,... | collective-permute-start | bytes 294920 | tf_op jit(solution)/shard_map/ppermute | solution.py:17
  81.1 1.3 collective-permute-start.1
  82.4 1.3 fusion.102
  83.7 3.9 %collective-permute-done.1 = bf16[96,1,4,1,128]{4,0,3,2,1:T(8,128)(2,1)S(1)} collective-permute-done((bf16[96,1,4,1,128]{4,0,3,2,1:T(8,128)(2,1)S(1)}, bf16[96,1,4,1,128]{4,0,3,2,1:T(8,128)(2,1)S(1)}, u32[]{:S(2)}, u32[]{:S(2)}) %collective-permute-start.1) | collective-permute-done | bytes 98336 | tf_op jit(solution)/shard_map/ppermute | solution.py:18
  87.6 0.4 fusion.41
  90.4 1.1 fusion.19
  92.1 1.2 fusion.25
  93.3 1.2 fusion.31
  94.5 1.3 copy-done.1
  96.1 2.8 %fusion.11 = f32[4,2,128,384]{2,3,1,0:T(8,128)S(1)} fusion(bf16[864,384,1,1]{1,0,3,2:T(8,128)(2,1)} %bitcast.175, bf16[864,1,4,2,128]{4,0,3,2,1:T(8,128)(2,1)} %copy-done.9), kind=kOutput, calls=%fused_computation.14 | convolution fusion | flops 679477248 | bytes 4005888 | tf_op jit(solution)/shard_map/dot_general | solution.py:140
  98.9 1.0 fusion.15
  100.0 0.4 copy-done.3
  100.4 2.0 %fusion.34 = bf16[384,1,4,2,128]{4,0,3,2,1:T(8,128)(2,1)} fusion(bf16[864,384,1,1]{1,0,3,2:T(8,128)(2,1)S(1)} %bitcast.169, bf16[864,1,4,2,128]{4,0,3,2,1:T(8,128)(2,1)S(1)} %copy-done.3, f32[4,2,128,384]{2,3,1,0:T(8,128)S(1)} %fusion.15, f32[4,2,128,384]{2,3,1,0:T(8,128)S(1)} %fusion.11), kind=kOutput, calls=%fused_computation.26 | convolution fusion | flops 680656896 | bytes 6365184 | tf_op jit(solution)/shard_map/dot_general | solution.py:140
  102.4 54.7 %all-reduce.6.cloned.1.call-done = bf16[3,3,3,96,384]{4,3,2,1,0:T(8,128)(2,1)} async-done(((bf16[3,3,3,96,384]{4,3,2,1,0:T(8,128)(2,1)}), bf16[3,3,3,96,384]{4,3,2,1,0:T(8,128)(2,1)}) %all-reduce.6.cloned.1.call-update) | async-done | bytes 1990672 | tf_op jit(solution)/shard_map/psum | solution.py:167
  157.1 4.0 %convert_element_type.145 = f32[3,3,3,96,384]{4,3,2,1,0:T(8,128)} convert(bf16[3,3,3,96,384]{4,3,2,1,0:T(8,128)(2,1)} %all-reduce.6.cloned.1.call-done) | non-fusion elementwise | flops 995328 | bytes 5971968 | tf_op jit(solution)/shard_map/convert_element_type | solution.py:167
  161.1 1.1 fusion.71
  162.1 0.8 copy.40
  (84 shorter events, 6.1 us)
Async XLA Ops:
  8.0 34.6 %copy-start = (bf16[384,384]{1,0:T(8,128)(2,1)S(1)}, bf16[384,384]{1,0:T(8,128)(2,1)}, u32[]{:S(2)}) copy-start(bf16[384,384]{1,0:T(8,128)(2,1)} %param.19) | copy-start | bytes 884740
  18.4 22.4 %slice-start = ((f32[1152]{0:T(1024)}), f32[384]{0:T(512)S(1)}, s32[]{:S(2)}) async-start(f32[1152]{0:T(1024)} %param.18), calls=%async_computation.5 | async-start | bytes 4096 | tf_op jit(solution)/shard_map/slice | solution.py:108
  18.4 11.8 %all-to-all-start = ((bf16[96,1,4,2,128]{4,0,3,1,2:T(8,128)(2,1)}), bf16[96,1,4,2,128]{4,0,3,1,2:T(8,128)(2,1)S(1)}, u32[]{:S(2)}, u32[]{:S(2)}) async-start(bf16[96,1,4,2,128]{4,0,3,1,2:T(8,128)(2,1)} %fusion.78), calls=%async_computation | async-start | bytes 393216 | tf_op jit(solution)/shard_map/all_to_all | solution.py:100
  31.8 10.8 %copy-start.15 = (f32[384]{0:T(512)S(1)}, f32[384]{0:T(512)}, u32[]{:S(2)}) copy-start(f32[384]{0:T(512)} %param.20) | copy-start | bytes 4612
  42.6 5.1 %copy-start.8 = (bf16[96,1,4,2,128]{4,3,2,1,0:T(2,128)(2,1)S(1)}, bf16[96,1,4,2,128]{4,3,2,1,0:T(2,128)(2,1)}, u32[]{:S(2)}) copy-start(bf16[96,1,4,2,128]{4,3,2,1,0:T(2,128)(2,1)} %param.25) | copy-start | bytes 589828
  42.6 11.3 %copy-start.5 = (bf16[96,1,4,2,128]{4,3,2,1,0:T(2,128)(2,1)S(1)}, bf16[96,1,4,2,128]{4,3,2,1,0:T(2,128)(2,1)}, u32[]{:S(2)}) copy-start(bf16[96,1,4,2,128]{4,3,2,1,0:T(2,128)(2,1)} %param.13) | copy-start | bytes 589828
  43.2 34.1 %copy-start.12 = (f32[96]{0:T(128)S(1)}, f32[96]{0:T(128)}, u32[]{:S(2)}) copy-start(f32[96]{0:T(128)} %param.22) | copy-start | bytes 1156
  43.3 34.1 %copy-start.13 = (f32[96]{0:T(128)S(1)}, f32[96]{0:T(128)}, u32[]{:S(2)}) copy-start(f32[96]{0:T(128)} %param.21) | copy-start | bytes 1156
  44.1 38.3 %copy-start.4 = (bf16[3,3,3,96,384]{4,3,2,1,0:T(8,128)(2,1)S(1)}, bf16[3,3,3,96,384]{4,3,2,1,0:T(8,128)(2,1)}, u32[]{:S(2)}) copy-start(bf16[3,3,3,96,384]{4,3,2,1,0:T(8,128)(2,1)} %param.23) | copy-start | bytes 5971972
  44.1 9.8 %all-to-all-start.1 = ((bf16[384,1,1,2,128]{4,3,2,1,0:T(2,128)(2,1)}), bf16[384,1,1,2,128]{4,3,2,1,0:T(2,128)(2,1)S(1)}, u32[]{:S(2)}, u32[]{:S(2)}) async-start(bf16[384,1,1,2,128]{4,3,2,1,0:T(2,128)(2,1)} %copy.33), calls=%async_computation.1 | async-start | bytes 393216 | tf_op jit(solution)/shard_map/all_to_all | solution.py:126
  47.6 109.4 %all-reduce.6.cloned.1.call-start = ((), (), s32[]{:S(2)}) async-start(), calls=%async_computation.4 | async-start | bytes 3981312 | tf_op jit(solution)/shard_map/psum | solution.py:167
  77.7 6.1 %collective-permute-start = (bf16[96,1,4,1,128]{4,0,3,2,1:T(8,128)(2,1)S(1)}, bf16[96,1,4,1,128]{4,0,3,2,1:T(8,128)(2,1)S(1)}, u32[]{:S(2)}, u32[]{:S(2)}) collective-permute-start(bf16[96,1,4,1,128]{4,0,3,2,1:T(8,128)(2,1)S(1)} %get-tuple-element.47), channel_id=1, source_target_pairs={{0,4},{1,5},{2,6},{3,7},{8,12},{9,13},{10,14},{11,15},{16,20},{17,... | collective-permute-start | bytes 294920 | tf_op jit(solution)/shard_map/ppermute | solution.py:17
  81.1 6.5 %collective-permute-start.1 = (bf16[96,1,4,1,128]{4,0,3,2,1:T(8,128)(2,1)S(1)}, bf16[96,1,4,1,128]{4,0,3,2,1:T(8,128)(2,1)S(1)}, u32[]{:S(2)}, u32[]{:S(2)}) collective-permute-start(bf16[96,1,4,1,128]{4,0,3,2,1:T(8,128)(2,1)S(1)} %get-tuple-element.48), channel_id=1, source_target_pairs={{4,0},{5,1},{6,2},{7,3},{12,8},{13,9},{14,10},{15,11},{20,16},{21,... | collective-permute-start | bytes 294920 | tf_op jit(solution)/shard_map/ppermute | solution.py:18
  89.2 1.1 copy-start.6
  90.3 1.2 copy-start.10
  90.3 1.8 %copy-start.9 = (bf16[864,1,4,2,128]{4,0,3,2,1:T(8,128)(2,1)}, bf16[864,1,4,2,128]{4,0,3,2,1:T(8,128)(2,1)S(1)}, u32[]{:S(2)}) copy-start(bf16[864,1,4,2,128]{4,0,3,2,1:T(8,128)(2,1)S(1)} %get-tuple-element.24) | copy-start | bytes 5308420
  91.9 1.4 copy-start.2
  94.5 1.3 copy-start.1
  95.8 65.2 %reduce-scatter.2.cloned.1.call-start = ((), (), s32[]{:S(2)}) async-start(), calls=%async_computation.3 | async-start | bytes 983040 | tf_op jit(solution)/shard_map/reduce_scatter | solution.py:143
  96.1 2.8 %copy-start.7 = (bf16[1,3,3,96,384]{4,3,2,1,0:T(8,128)(2,1)S(1)}, bf16[1,3,3,96,384]{4,3,2,1,0:T(8,128)(2,1)}, u32[]{:S(2)}) copy-start(bf16[1,3,3,96,384]{4,3,2,1,0:T(8,128)(2,1)} %get-tuple-element.22) | copy-start | bytes 1990660
  96.1 2.8 %copy-start.11 = (bf16[864,1,4,2,128]{4,0,3,2,1:T(8,128)(2,1)S(1)}, bf16[864,1,4,2,128]{4,0,3,2,1:T(8,128)(2,1)}, u32[]{:S(2)}) copy-start(bf16[864,1,4,2,128]{4,0,3,2,1:T(8,128)(2,1)} %copy-done.10) | copy-start | bytes 5308420
  98.9 1.5 copy-start.3
  102.4 58.7 %copy-start.14 = (f32[96]{0:T(128)S(1)}, f32[96]{0:T(128)}, u32[]{:S(2)}) copy-start(f32[96]{0:T(128)} %param.24) | copy-start | bytes 1156
Sparse Core Ops, SparseCore 0:
  96.0 61.0 all-reduce.5
Sparse Core Ops, SparseCore 1:
  102.5 22.9 reduce-scatter.1
where the time goes:
time: 171 us; the launch traced here: 170 us
  waiting for transfers between devices  70.3 us (41%)
  blocking collectives  37 us (22%)
  between operations  16.6 us (10%)
  starting transfers between devices  14 us (8%)
  matrix products  13.4 us (8%)
  other arithmetic  10.1 us (6%)
  local copies, waits for them, and re-layouts  9.05 us (5%)
    psum x1, waiting for transfers between devices, body(): lax.psum(grad_table.astype(jnp.bfloat16), ('ha', 'dp')).astype(jnp.float32)  54.7 us
    all_gather x1, blocking collectives, body(): piece = lax.all_gather(masked_cot, 'ch', axis=0, tiled=True)  17.3 us
    psum x2, blocking collectives, body(): first, second = lax.psum((first, second), 'ha')  10.8 us
    all_gather x1, blocking collectives, body(): piece = lax.all_gather(pairs, 'ha', axis=1, tiled=True)  8.94 us
    all_to_all x1, waiting for transfers between devices, body(): lax.all_to_all(projected, 'ch', split_axis=0, concat_axis=2, tiled=True)  6.12 us
    dot_general x3, matrix products, body(): lax.dot_general(part, stacks[time_tap], (((0,), (0,)), ((), ())), preferr...  5.78 us
    all_to_all x1, waiting for transfers between devices, body(): lax.all_to_all(normed, 'ch', split_axis=2, concat_axis=0, tiled=True)  5.55 us
    all_to_all x1, starting transfers between devices, body(): lax.all_to_all(normed, 'ch', split_axis=2, concat_axis=0, tiled=True)  5.54 us
  transfers between devices with their start and end apart: 6, of which 4 were waited for; matrix products, arithmetic and copies ran while one was open for 7% of the time, Pallas kernels for 0%

commit v1 on v0

--- a/solution.py
+++ b/solution.py
@@ -164,7 +164,9 @@
         )
     grad_table = carry
     grad_table = grad_table.reshape(3, 3, 3, chans, full_width)
-    weight_grad = lax.psum(grad_table.astype(jnp.bfloat16), ("ha", "dp")).astype(jnp.float32)
+    weight_grad = jnp.sum(
+        lax.all_gather(grad_table.astype(jnp.bfloat16), ("ha", "dp")), axis=0
+    ).astype(jnp.float32)
     return (mixed, weight_grad)
 
 

time: 171 us -> 211 us (1.23)
  waiting for transfers between devices: 70.3 us -> 94.9 us
  blocking collectives: 37 us -> 51.2 us
  other arithmetic: 10.1 us -> 17.8 us
  starting transfers between devices: 14 us -> 10.3 us
    all_gather x0 -> x1, waiting for transfers between devices: none -> 84.3 us  [body(): lax.all_gather(grad_table.astype(jnp.bfloat16), ('ha', 'dp'))]
    psum x1 -> x0, waiting for transfers between devices: 54.7 us -> none  [body(): lax.psum(grad_table.astype(jnp.bfloat16), ('ha', 'dp')).astype(jnp.float32)]
    all_to_all x0 -> x1, blocking collectives: none -> 9.99 us  [body(): lax.all_to_all(projected, 'ch', split_axis=0, concat_axis=2, tiled=True)]
    reduce_sum x0 -> x1, other arithmetic: none -> 9.22 us  [body(): jnp.sum(lax.all_gather(grad_table.astype(jnp.bfloat16), ('ha', 'dp')), ax...]
    all_to_all x1 -> x0, waiting for transfers between devices: 6.12 us -> none  [body(): lax.all_to_all(projected, 'ch', split_axis=0, concat_axis=2, tiled=True)]
    all_gather x1, blocking collectives: 17.3 us -> 21.5 us  [body(): piece = lax.all_gather(masked_cot, 'ch', axis=0, tiled=True)]
    all_to_all x1 -> x0, starting transfers between devices: 3.5 us -> none  [body(): lax.all_to_all(projected, 'ch', split_axis=0, concat_axis=2, tiled=True)]
    unnamed x41 -> x35, local copies, waits for them, and re-layouts: 4.48 us -> 5.44 us
  transfers between devices with their start and end apart: 6 -> 5, of which waited for: 4 -> 4; matrix products, arithmetic and copies ran while one was open for 7% -> 3% of each run, Pallas kernels for 0% -> 0%
where the time goes in v1:
time: 211 us
  waiting for transfers between devices  94.9 us (45%)
  blocking collectives  51.2 us (24%)
  other arithmetic  17.8 us (8%)
  between operations  16.6 us (8%)
  matrix products  11.6 us (5%)
  starting transfers between devices  10.3 us (5%)
  local copies, waits for them, and re-layouts  8.19 us (4%)
    all_gather x1, waiting for transfers between devices, body(): lax.all_gather(grad_table.astype(jnp.bfloat16), ('ha', 'dp'))  84.3 us
    all_gather x1, blocking collectives, body(): piece = lax.all_gather(masked_cot, 'ch', axis=0, tiled=True)  21.5 us
    psum x2, blocking collectives, body(): first, second = lax.psum((first, second), 'ha')  10.8 us
    all_to_all x1, blocking collectives, body(): lax.all_to_all(projected, 'ch', split_axis=0, concat_axis=2, tiled=True)  9.99 us
    reduce_sum x1, other arithmetic, body(): jnp.sum(lax.all_gather(grad_table.astype(jnp.bfloat16), ('ha', 'dp')), ax...  9.22 us
    all_gather x1, blocking collectives, body(): piece = lax.all_gather(pairs, 'ha', axis=1, tiled=True)  8.94 us
    all_to_all x1, waiting for transfers between devices, body(): lax.all_to_all(normed, 'ch', split_axis=2, concat_axis=0, tiled=True)  5.55 us
    all_to_all x1, starting transfers between devices, body(): lax.all_to_all(normed, 'ch', split_axis=2, concat_axis=0, tiled=True)  5.54 us
  transfers between devices with their start and end apart: 5, of which 4 were waited for; matrix products, arithmetic and copies ran while one was open for 3% of the time, Pallas kernels for 0%

profile of v1, /device:TPU:0, one launch (start us, length us, event | category | flops | bytes accessed | tf_op | source)
XLA Modules:
  0.0 210.5 jit_solution(9611777551556357532)
XLA Ops:
  8.7 1.1 fusion.57
  10.4 5.9 %all-reduce.3 = (f32[8,1]{0,1:T(1,128)S(1)}, f32[8,1]{0,1:T(1,128)S(1)}) all-reduce(f32[8,1]{0,1:T(1,128)S(1)} %convolution_bitcast_fusion.3, f32[8,1]{0,1:T(1,128)S(1)} %convolution_bitcast_fusion.2), channel_id=1, replica_groups=mesh['ch'=4,'ha'=2,'dp'=4] {'ha'}, use_global_device_ids=true, to_apply=%region_2.0 | all-reduce | flops 16 | bytes 128 | tf_op jit(solution)/shard_map/psum | solution.py:96
  16.6 1.8 fusion.78
  18.4 5.5 %all-to-all-start = ((bf16[96,1,4,2,128]{4,0,3,1,2:T(8,128)(2,1)}), bf16[96,1,4,2,128]{4,0,3,1,2:T(8,128)(2,1)S(1)}, u32[]{:S(2)}, u32[]{:S(2)}) async-start(bf16[96,1,4,2,128]{4,0,3,1,2:T(8,128)(2,1)} %fusion.78), calls=%async_computation | async-start | bytes 393216 | tf_op jit(solution)/shard_map/all_to_all | solution.py:100
  24.0 0.7 slice.120
  24.7 5.5 %all-to-all-done = bf16[96,1,4,2,128]{4,0,3,1,2:T(8,128)(2,1)S(1)} async-done(((bf16[96,1,4,2,128]{4,0,3,1,2:T(8,128)(2,1)}), bf16[96,1,4,2,128]{4,0,3,1,2:T(8,128)(2,1)S(1)}, u32[]{:S(2)}, u32[]{:S(2)}) %all-to-all-start) | async-done | bytes 196640 | tf_op jit(solution)/shard_map/all_to_all | solution.py:100
  30.4 1.5 fusion.37
  31.8 8.9 %all-gather = bf16[512,768]{1,0:T(8,128)(2,1)S(1)} all-gather(bf16[256,768]{1,0:T(8,128)(2,1)S(1)} %fusion.37), channel_id=2, replica_groups=mesh['ch'=4,'ha'=2,'dp'=4] {'ha'}, dimensions={0}, use_global_device_ids=true | all-gather | bytes 1179648 | tf_op jit(solution)/shard_map/all_gather | solution.py:119
  40.8 1.6 fusion.104
  42.7 0.6 fusion.46
  43.4 10.0 %all_to_all.24 = bf16[384,1,1,2,128]{4,3,2,1,0:T(2,128)(2,1)S(1)} all-to-all(bf16[384,1,1,2,128]{4,3,2,1,0:T(2,128)(2,1)S(1)} %copy.33), channel_id=1, replica_groups=mesh['ch'=4,'ha'=2,'dp'=4] {'ch'}, dimensions={0} | all-to-all | bytes 393216 | tf_op jit(solution)/shard_map/all_to_all | solution.py:126
  54.3 4.9 %all-reduce.2 = (f32[8,1]{0,1:T(1,128)S(1)}, f32[8,1]{0,1:T(1,128)S(1)}) all-reduce(f32[8,1]{0,1:T(1,128)S(1)} %convolution_bitcast_fusion.1, f32[8,1]{0,1:T(1,128)S(1)} %convolution_bitcast_fusion), channel_id=1, replica_groups=mesh['ch'=4,'ha'=2,'dp'=4] {'ha'}, use_global_device_ids=true, to_apply=%region_10.11 | all-reduce | flops 16 | bytes 128 | tf_op jit(solution)/shard_map/psum | solution.py:129
  59.9 3.5 %collective-permute-start = (bf16[96,1,4,1,128]{4,0,3,2,1:T(8,128)(2,1)S(1)}, bf16[96,1,4,1,128]{4,0,3,2,1:T(8,128)(2,1)S(1)}, u32[]{:S(2)}, u32[]{:S(2)}) collective-permute-start(bf16[96,1,4,1,128]{4,0,3,2,1:T(8,128)(2,1)S(1)} %get-tuple-element.47), channel_id=1, source_target_pairs={{0,4},{1,5},{2,6},{3,7},{8,12},{9,13},{10,14},{11,15},{16,20},{17,... | collective-permute-start | bytes 294920 | tf_op jit(solution)/shard_map/ppermute | solution.py:17
  63.4 1.3 collective-permute-start.1
  64.9 0.7 collective-permute-done
  65.6 4.3 %collective-permute-done.1 = bf16[96,1,4,1,128]{4,0,3,2,1:T(8,128)(2,1)S(1)} collective-permute-done((bf16[96,1,4,1,128]{4,0,3,2,1:T(8,128)(2,1)S(1)}, bf16[96,1,4,1,128]{4,0,3,2,1:T(8,128)(2,1)S(1)}, u32[]{:S(2)}, u32[]{:S(2)}) %collective-permute-start.1) | collective-permute-done | bytes 98336 | tf_op jit(solution)/shard_map/ppermute | solution.py:18
  69.9 0.4 fusion.41
  71.7 0.4 constant_dynamic-update-slice_fusion
  72.9 1.0 fusion.15
  73.9 1.0 fusion.11
  75.0 2.0 fusion.34
  77.1 21.5 %all_gather.11 = bf16[384,1,4,2,128]{4,0,3,2,1:T(8,128)(2,1)S(1)} all-gather(bf16[96,1,4,2,128]{4,0,3,2,1:T(8,128)(2,1)S(1)} %copy_multiply_fusion), channel_id=1, replica_groups=mesh['ch'=4,'ha'=2,'dp'=4] {'ch'}, dimensions={0}, use_global_device_ids=true | all-gather | bytes 983040 | tf_op jit(solution)/shard_map/all_gather | solution.py:153
  98.6 1.1 fusion.19
  99.9 1.3 copy-done.8
  101.2 1.2 fusion.25
  102.7 1.2 fusion.31
  103.9 1.3 copy-done.1
  105.3 1.1 fusion.71
  106.3 0.8 copy.40
  107.2 84.3 %all-gather.3.cloned.1.call-done = bf16[8,3,3,3,96,384]{5,4,3,2,1,0:T(8,128)(2,1)} async-done(((bf16[1,3,3,3,96,384]{5,4,3,2,1,0:T(8,128)(2,1)}), bf16[8,3,3,3,96,384]{5,4,3,2,1,0:T(8,128)(2,1)}) %all-gather.3.cloned.1.call-update) | async-done | bytes 15925264 | tf_op jit(solution)/shard_map/all_gather | solution.py:168
  191.4 9.2 %reduce_sum.98 = bf16[3,3,3,96,384]{4,3,2,1,0:T(8,128)(2,1)S(1)} reduce(bf16[8,3,3,3,96,384]{5,4,3,2,1,0:T(8,128)(2,1)} %all-gather.3.cloned.1.call-done, bf16[]{:T(256)} %constant.6.clone.1), dimensions={0}, to_apply=%region_15.16 | reduce | flops 6967296 | bytes 17915906 | tf_op jit(solution)/shard_map/reduce_sum | solution.py:167
  200.6 2.4 %convert_element_type.154 = f32[3,3,3,96,384]{4,3,2,1,0:T(8,128)} convert(bf16[3,3,3,96,384]{4,3,2,1,0:T(8,128)(2,1)S(1)} %reduce_sum.98) | non-fusion elementwise | flops 995328 | bytes 5971968 | tf_op jit(solution)/shard_map/convert_element_type | solution.py:169
  (78 shorter events, 6.0 us)
Async XLA Ops:
  8.0 34.6 %copy-start = (bf16[384,384]{1,0:T(8,128)(2,1)S(1)}, bf16[384,384]{1,0:T(8,128)(2,1)}, u32[]{:S(2)}) copy-start(bf16[384,384]{1,0:T(8,128)(2,1)} %param.19) | copy-start | bytes 884740
  18.4 22.4 %slice-start = ((f32[1152]{0:T(1024)}), f32[384]{0:T(512)S(1)}, s32[]{:S(2)}) async-start(f32[1152]{0:T(1024)} %param.18), calls=%async_computation.5 | async-start | bytes 4096 | tf_op jit(solution)/shard_map/slice | solution.py:108
  18.4 11.8 %all-to-all-start = ((bf16[96,1,4,2,128]{4,0,3,1,2:T(8,128)(2,1)}), bf16[96,1,4,2,128]{4,0,3,1,2:T(8,128)(2,1)S(1)}, u32[]{:S(2)}, u32[]{:S(2)}) async-start(bf16[96,1,4,2,128]{4,0,3,1,2:T(8,128)(2,1)} %fusion.78), calls=%async_computation | async-start | bytes 393216 | tf_op jit(solution)/shard_map/all_to_all | solution.py:100
  24.0 81.3 %reduce-scatter.2.cloned.1.call-start = ((), (), s32[]{:S(2)}) async-start(), calls=%async_computation.3 | async-start | bytes 983040 | tf_op jit(solution)/shard_map/reduce_scatter | solution.py:143
  31.8 10.8 %copy-start.12 = (f32[384]{0:T(512)S(1)}, f32[384]{0:T(512)}, u32[]{:S(2)}) copy-start(f32[384]{0:T(512)} %param.20) | copy-start | bytes 4612
  42.6 10.8 %copy-start.5 = (bf16[96,1,4,2,128]{4,3,2,1,0:T(2,128)(2,1)S(1)}, bf16[96,1,4,2,128]{4,3,2,1,0:T(2,128)(2,1)}, u32[]{:S(2)}) copy-start(bf16[96,1,4,2,128]{4,3,2,1,0:T(2,128)(2,1)} %param.13) | copy-start | bytes 589828
  42.6 16.9 %copy-start.9 = (f32[96]{0:T(128)S(1)}, f32[96]{0:T(128)}, u32[]{:S(2)}) copy-start(f32[96]{0:T(128)} %param.22) | copy-start | bytes 1156
  42.7 16.9 %copy-start.10 = (f32[96]{0:T(128)S(1)}, f32[96]{0:T(128)}, u32[]{:S(2)}) copy-start(f32[96]{0:T(128)} %param.21) | copy-start | bytes 1156
  43.3 21.4 %copy-start.4 = (bf16[3,3,3,96,384]{4,3,2,1,0:T(8,128)(2,1)S(1)}, bf16[3,3,3,96,384]{4,3,2,1,0:T(8,128)(2,1)}, u32[]{:S(2)}) copy-start(bf16[3,3,3,96,384]{4,3,2,1,0:T(8,128)(2,1)} %param.23) | copy-start | bytes 5971972
  59.9 5.7 %collective-permute-start = (bf16[96,1,4,1,128]{4,0,3,2,1:T(8,128)(2,1)S(1)}, bf16[96,1,4,1,128]{4,0,3,2,1:T(8,128)(2,1)S(1)}, u32[]{:S(2)}, u32[]{:S(2)}) collective-permute-start(bf16[96,1,4,1,128]{4,0,3,2,1:T(8,128)(2,1)S(1)} %get-tuple-element.47), channel_id=1, source_target_pairs={{0,4},{1,5},{2,6},{3,7},{8,12},{9,13},{10,14},{11,15},{16,20},{17,... | collective-permute-start | bytes 294920 | tf_op jit(solution)/shard_map/ppermute | solution.py:17
  63.4 6.5 %collective-permute-start.1 = (bf16[96,1,4,1,128]{4,0,3,2,1:T(8,128)(2,1)S(1)}, bf16[96,1,4,1,128]{4,0,3,2,1:T(8,128)(2,1)S(1)}, u32[]{:S(2)}, u32[]{:S(2)}) collective-permute-start(bf16[96,1,4,1,128]{4,0,3,2,1:T(8,128)(2,1)S(1)} %get-tuple-element.48), channel_id=1, source_target_pairs={{4,0},{5,1},{6,2},{7,3},{12,8},{13,9},{14,10},{15,11},{20,16},{21,... | collective-permute-start | bytes 294920 | tf_op jit(solution)/shard_map/ppermute | solution.py:18
  72.7 1.2 copy-start.7
  72.9 2.1 copy-start.2
  75.0 2.1 copy-start.6
  77.0 114.4 %all-gather.3.cloned.1.call-start = ((), (), s32[]{:S(2)}) async-start(), calls=%async_computation.4 | async-start | bytes 17915904 | tf_op jit(solution)/shard_map/all_gather | solution.py:168
  99.7 1.5 copy-start.8
  101.2 1.5 copy-start.3
  103.9 1.3 copy-start.1
  103.9 1.3 copy-start.11
Sparse Core Ops, SparseCore 0:
  77.1 25.7 reduce-scatter.1
Sparse Core Ops, SparseCore 1:
  105.3 86.1 all-gather.2
